TPU v7x, 256 devices: a whole 4x4x8 slice. The times are simulated.
256 devices in a mesh: band: 64 (over z_lo, x, y, core), sector: 4 (over z_hi).
Axes of the slice: x: 4, y: 4, z: 8 (z_hi: 4, z_lo: 2; z = z_hi * 2 + z_lo), core: 2. Of those that a mesh axis runs over, the one named last changes fastest.
Arguments:
- field: bfloat16 [64, 1440, 72], P('band', 'sector'), may hold values from -6 to 6
- filters: float32 [9, 64, 3, 17], P(None, 'band'), may hold values from -1.2 to 1.2
- reach: int32 [64], P('band'), may hold values from 1 to 8, as said below
- w_enc: bfloat16 [9, 72, 384], replicated, may hold values from -0.25 to 0.25
- gain: float32 [384], replicated, may hold values from 0.5 to 1.5
- w_qkv: bfloat16 [384, 1152], replicated, may hold values from -0.3125 to 0.3125
- w_out: bfloat16 [384, 384], replicated, may hold values from -0.3125 to 0.3125
- tau: float32 [8], replicated, may hold values from 0.25 to 24
- neighbours: int32 [64, 4, 3, 4], P('band', 'sector'), may hold values from 0 to 1, as said below
Outputs:
- output: bfloat16 [64, 1440, 384], P('band', 'sector')
Inputs may be any that keep to these rules, and one draw needn't show every extreme that they name: reach[i] is the filter's longitude reach in row i; it equals 8 in the first and last row. neighbours[b, s, r, t] is 1 where query block (b, s) attends key row b - 1 + r in sector t; it is 1 for the block's own rows in its own sector and 0 for rows outside the grid.
All inputs are finite; a program needn't handle non-finite values.
Results may differ from a plain program's by a relative error of at most 0.03.
Values may be sent and summed in bfloat16 or wider, within the bound.
No kernel may reach another device: no remote copies, remote signals or barrier semaphores. Data moves between devices by JAX's collectives and lax.ppermute only.
A program may use at most 64 MiB of HBM per device.

v0:
```python
import math
import jax
import jax.numpy as jnp
from jax import lax
from jax.sharding import PartitionSpec as P

HEADS = 8
FR = 1
LW = 8
KH = 1


def padded(block, sides, width, periodic):
    for axis, dim in sides:
        count = lax.axis_size(axis)
        forward = [(i, i + 1) for i in range(count - 1)]
        if periodic:
            forward.append((count - 1, 0))
        backward = [(target, source) for source, target in forward]
        low = lax.ppermute(
            lax.slice_in_dim(block, block.shape[dim] - width, None, axis=dim), axis, forward
        )
        high = lax.ppermute(lax.slice_in_dim(block, 0, width, axis=dim), axis, backward)
        block = jnp.concatenate([low, block, high], axis=dim)
    return block


def rotate(values, row_ids, col_ids, nlat, nlon):
    npair = values.shape[-1] // 2
    nhalf = npair // 2
    index = jnp.arange(npair, dtype=jnp.int32)
    lon_freq = jnp.where(index < nhalf, index + 1, 0).astype(jnp.float32)
    lat_freq = jnp.where(index >= nhalf, index - nhalf + 1, 0).astype(jnp.float32)
    lon_angle = 2.0 * math.pi / nlon * col_ids.astype(jnp.float32)
    lat_angle = math.pi / nlat * (row_ids.astype(jnp.float32) + 0.5)
    angle = lat_angle[:, None, None] * lat_freq + lon_angle[None, :, None] * lon_freq
    cosine = jnp.cos(angle)[:, :, None, :]
    sine = jnp.sin(angle)[:, :, None, :]
    first = values[..., :npair]
    second = values[..., npair:]
    return jnp.concatenate([first * cosine - second * sine, first * sine + second * cosine], -1)


def normalize(hidden, gain):
    values = hidden.astype(jnp.float32)
    meansquare = jnp.mean(values * values, -1, keepdims=True)
    return (values * lax.rsqrt(meansquare + 1e-05) * gain).astype(jnp.bfloat16)


def spread(payload):
    cycle_cells = lax.all_gather(payload, "sector", axis=1, tiled=True)
    return padded(cycle_cells, (("band", 0),), KH, False)


def local(field, filters, reach, w_enc, gain, w_qkv, w_out, tau, neighbours):
    rows_dev, lon_dev, channels = field.shape
    d_model = gain.shape[0]
    head_dim = d_model // HEADS
    nlat = rows_dev * lax.axis_size("band")
    nlon = lon_dev * lax.axis_size("sector")
    row_start = lax.axis_index("band") * rows_dev
    col_start = lax.axis_index("sector") * lon_dev
    side_cells = padded(field, (("sector", 1),), LW, True)
    block_cells = padded(side_cells, (("band", 0),), FR, False)
    offsets = jnp.abs(jnp.arange(2 * LW + 1, dtype=jnp.int32) - LW)
    tap_keep = (offsets[None, :] <= reach[:, None]).astype(jnp.float32)
    tap_weights = filters * tap_keep[None, :, None, :]
    shifted = jnp.stack(
        [
            jnp.stack(
                [
                    block_cells[above : above + rows_dev, shift : shift + lon_dev]
                    for shift in range(2 * LW + 1)
                ],
                1,
            )
            for above in range(2 * FR + 1)
        ],
        1,
    )
    conv = jnp.einsum(
        "kiab,iabjc->kijc",
        tap_weights,
        shifted.astype(jnp.float32),
        precision=lax.Precision.HIGHEST,
    ).astype(jnp.bfloat16)
    hidden = jax.nn.gelu(
        jnp.einsum("kijc,kcd->ijd", conv, w_enc, preferred_element_type=jnp.float32)
    ).astype(jnp.bfloat16)
    own_rows = row_start + jnp.arange(rows_dev, dtype=jnp.int32)
    own_cols = col_start + jnp.arange(lon_dev, dtype=jnp.int32)
    normed = normalize(hidden, gain).reshape(rows_dev * lon_dev, d_model)
    proj = jnp.dot(normed, w_qkv, preferred_element_type=jnp.float32)
    proj = proj.reshape(rows_dev, lon_dev, 3, HEADS, head_dim)
    query = rotate(proj[:, :, 0], own_rows, own_cols, nlat, nlon).astype(jnp.bfloat16)
    key_own = rotate(proj[:, :, 1], own_rows, own_cols, nlat, nlon).astype(jnp.bfloat16)
    value_own = proj[:, :, 2].astype(jnp.bfloat16)
    payload = jnp.concatenate(
        [
            key_own.reshape(rows_dev, lon_dev, d_model),
            value_own.reshape(rows_dev, lon_dev, d_model),
        ],
        -1,
    )
    gathered = spread(payload)
    key_rows = gathered.shape[0]
    key_all = gathered[..., :d_model].reshape(key_rows, nlon, HEADS, head_dim)
    value_all = gathered[..., d_model:].reshape(key_rows, nlon, HEADS, head_dim)
    keymask = jnp.repeat(neighbours[0, 0], lon_dev, axis=1).reshape(-1) > 0
    queries = jnp.transpose(query.reshape(rows_dev * lon_dev, HEADS, head_dim), (1, 0, 2))
    key_heads = jnp.transpose(key_all.reshape(key_rows * nlon, HEADS, head_dim), (1, 0, 2))
    value_heads = jnp.transpose(value_all.reshape(key_rows * nlon, HEADS, head_dim), (1, 0, 2))
    inv_root = 1.0 / math.sqrt(head_dim)

    def one_head(operands):
        q_head, k_head, v_head, temper = operands
        scores = jnp.einsum("qd,kd->qk", q_head, k_head, preferred_element_type=jnp.float32)
        scores = scores * (temper * inv_root)
        scores = jnp.where(keymask[None, :], scores, -1e30)
        peak = jnp.max(scores, -1, keepdims=True)
        expo = jnp.exp(scores - peak)
        total = jnp.sum(expo, -1, keepdims=True)
        summed = jnp.dot(expo.astype(jnp.bfloat16), v_head, preferred_element_type=jnp.float32)
        return summed / total

    attended = lax.map(one_head, (queries, key_heads, value_heads, tau))
    attended = (
        jnp.transpose(attended, (1, 0, 2)).reshape(rows_dev * lon_dev, d_model).astype(jnp.bfloat16)
    )
    mixed = jnp.dot(attended, w_out, preferred_element_type=jnp.float32).reshape(
        rows_dev, lon_dev, d_model
    )
    return (hidden.astype(jnp.float32) + mixed).astype(jnp.bfloat16)


def solution(mesh):
    return jax.shard_map(
        local,
        mesh=mesh,
        in_specs=(
            P("band", "sector", None),
            P(None, "band", None, None),
            P("band"),
            P(),
            P(),
            P(),
            P(),
            P(),
            P("band", "sector", None, None),
        ),
        out_specs=P("band", "sector", None),
        check_vma=False,
    )
```

profile of v0, /device:TPU:31, one launch (start us, length us, event | category | flops | bytes accessed | tf_op | source)
XLA Modules:
  0.0 237.7 jit_solution(11369777460939733356)
XLA Ops:
  7.4 3.0 %collective-permute-start = (bf16[1,8,72]{1,2,0:T(8,128)(2,1)S(1)}, bf16[1,8,72]{1,2,0:T(8,128)(2,1)S(1)}, u32[]{:S(2)}, u32[]{:S(2)}) collective-permute-start(bf16[1,8,72]{1,2,0:T(8,128)(2,1)S(1)} %get-tuple-element.317), channel_id=1, source_target_pairs={{0,1},{1,2},{2,3},{3,0},{4,5},{5,6},{6,7},{7,4},{8,9},{9,10},{10,1... | collective-permute-start | bytes 3464 | tf_op jit(solution)/shard_map/ppermute | solution.py:20
  10.4 3.1 %collective-permute-start.1 = (bf16[1,8,72]{1,2,0:T(8,128)(2,1)S(1)}, bf16[1,8,72]{1,2,0:T(8,128)(2,1)S(1)}, u32[]{:S(2)}, u32[]{:S(2)}) collective-permute-start(bf16[1,8,72]{1,2,0:T(8,128)(2,1)S(1)} %get-tuple-element.318), channel_id=1, source_target_pairs={{1,0},{2,1},{3,2},{0,3},{5,4},{6,5},{7,6},{4,7},{9,8},{10,9},{11,1... | collective-permute-start | bytes 3464 | tf_op jit(solution)/shard_map/ppermute | solution.py:23
  15.2 1.8 copy.1531
  17.9 3.1 %collective-permute-start.2 = (bf16[1,376,72]{1,2,0:T(8,128)(2,1)S(1)}, bf16[1,376,72]{1,2,0:T(8,128)(2,1)S(1)}, u32[]{:S(2)}, u32[]{:S(2)}) collective-permute-start(bf16[1,376,72]{1,2,0:T(8,128)(2,1)S(1)} %pad_maximum_fusion.4), channel_id=1, source_target_pairs={{0,4},{4,8},{8,12},{12,16},{16,20},{20,24},{24,28},{28,32},{32,36}... | collective-permute-start | bytes 162440 | tf_op jit(solution)/shard_map/ppermute | solution.py:20
  21.0 1.9 collective-permute-start.3
  23.8 0.9 constant_dynamic-update-slice_fusion.32
  24.7 0.9 constant_dynamic-update-slice_fusion.31
  36.4 2.3 fusion.30
  41.4 1.1 copy.1532
  42.5 52.8 %all-gather.2.cloned.1.call-done = bf16[1,1440,768]{2,1,0:T(8,128)(2,1)} async-done(((bf16[1,360,768]{2,1,0:T(8,128)(2,1)}), bf16[1,1440,768]{2,1,0:T(8,128)(2,1)}) %all-gather.2.cloned.1.call-update) | async-done | bytes 2211856 | tf_op jit(solution)/shard_map/all_gather | solution.py:51
  95.3 5.2 %collective-permute-start.4 = (bf16[1,1440,768]{2,1,0:T(8,128)(2,1)}, bf16[1,1440,768]{2,1,0:T(8,128)(2,1)}, u32[]{:S(2)}, u32[]{:S(2)}) collective-permute-start(bf16[1,1440,768]{2,1,0:T(8,128)(2,1)} %all-gather.2.cloned.1.call-done), channel_id=1, source_target_pairs={{0,4},{4,8},{8,12},{12,16},{16,20},{20,24},{24,28},{28,32},{32,36}... | collective-permute-start | bytes 6635528 | tf_op jit(solution)/shard_map/ppermute | solution.py:20
  100.5 2.1 collective-permute-start.5
  102.6 0.9 maximum_bitcast_fusion.6
  103.6 21.4 %collective-permute-done.4 = bf16[1,1440,768]{2,1,0:T(8,128)(2,1)} collective-permute-done((bf16[1,1440,768]{2,1,0:T(8,128)(2,1)}, bf16[1,1440,768]{2,1,0:T(8,128)(2,1)}, u32[]{:S(2)}, u32[]{:S(2)}) %collective-permute-start.4) | collective-permute-done | bytes 2211872 | tf_op jit(solution)/shard_map/ppermute | solution.py:20
  125.0 1.8 constant_dynamic-update-slice_fusion.53
  126.9 6.7 %collective-permute-done.5 = bf16[1,1440,768]{2,1,0:T(8,128)(2,1)} collective-permute-done((bf16[1,1440,768]{2,1,0:T(8,128)(2,1)}, bf16[1,1440,768]{2,1,0:T(8,128)(2,1)}, u32[]{:S(2)}, u32[]{:S(2)}) %collective-permute-start.5) | collective-permute-done | bytes 2211872 | tf_op jit(solution)/shard_map/ppermute | solution.py:23
  133.6 1.8 constant_dynamic-update-slice_fusion.51
  135.4 3.4 %fusion.90 = (bf16[3,1440,384]{2,1,0:T(8,128)(2,1)}, bf16[3,1440,384]{2,1,0:T(8,128)(2,1)}) fusion(bf16[3,1440,768]{2,1,0:T(8,128)(2,1)S(1)} %constant_dynamic-update-slice_fusion.51), kind=kLoop, calls=%fused_computation.220 | loop fusion | bytes 13271040 | tf_op jit(solution)/shard_map/slice | solution.py:108
  138.8 8.6 %copy.1533 = bf16[3,1440,384]{1,0,2:T(4,128)(2,1)} copy(bf16[3,1440,384]{2,1,0:T(8,128)(2,1)} %get-tuple-element.308) | data formatting | bytes 6635520 | tf_op jit(solution)/shard_map/slice | solution.py:107
  147.4 9.8 %reshape_reshape.7 = bf16[4320,8,48]{0,2,1:T(8,128)(2,1)} reshape(bf16[3,1440,384]{1,0,2:T(4,128)(2,1)} %copy.1533) | data formatting | bytes 6635520 | tf_op jit(solution)/shard_map/reshape;reshape | solution.py:111
  157.2 8.6 %copy.1534 = bf16[3,1440,384]{1,0,2:T(4,128)(2,1)} copy(bf16[3,1440,384]{2,1,0:T(8,128)(2,1)} %get-tuple-element.307) | data formatting | bytes 6635520 | tf_op jit(solution)/shard_map/slice | solution.py:108
  165.9 9.9 %reshape_reshape.8 = bf16[4320,8,48]{0,2,1:T(8,128)(2,1)} reshape(bf16[3,1440,384]{1,0,2:T(4,128)(2,1)} %copy.1534) | data formatting | bytes 6635520 | tf_op jit(solution)/shard_map/reshape;reshape | solution.py:112
  175.8 54.0 %while.11 = (s32[]{:T(128)}, bf16[8,360,48]{1,2,0:T(8,128)(2,1)S(1)}, bf16[8,360,48]{1,2,0:T(8,128)(2,1)S(1)}, bf16[8,4320,48]{1,2,0:T(8,128)(2,1)}, f32[8]{0:T(...) while((s32[]{:T(128)}, ...), condition=%wide.region_4.5_spmd.clone, body=%wide.region_1.4_spmd.clone.sunk | while | flops 309501376 | bytes 19683840 | solution.py:126
  177.2 2.1 fusion.103
  179.3 1.0 fusion.104
  180.3 2.2 fusion.105
  184.0 2.1 fusion.103
  186.1 1.0 fusion.104
  187.1 2.2 fusion.105
  190.7 2.1 fusion.103
  192.8 1.0 fusion.104
  193.8 2.2 fusion.105
  197.5 2.1 fusion.103
  199.6 1.0 fusion.104
  200.6 2.2 fusion.105
  204.2 2.1 fusion.103
  206.3 1.0 fusion.104
  207.3 2.2 fusion.105
  210.9 2.1 fusion.103
  213.1 1.0 fusion.104
  214.1 2.2 fusion.105
  217.7 2.1 fusion.103
  219.8 1.0 fusion.104
  220.8 2.2 fusion.105
  224.4 2.1 fusion.103
  226.6 1.0 fusion.104
  227.6 2.2 fusion.105
  229.8 1.1 fusion.32
  (118 shorter events, 23.1 us)
Async XLA Ops:
  6.5 32.2 %copy-start = (bf16[9,72,384]{2,1,0:T(8,128)(2,1)S(1)}, bf16[9,72,384]{2,1,0:T(8,128)(2,1)}, u32[]{:S(2)}) copy-start(bf16[9,72,384]{2,1,0:T(8,128)(2,1)} %param.14) | copy-start | bytes 1492996
  6.5 25.4 %copy-start.1 = (bf16[1,360,72]{1,2,0:T(8,128)(2,1)S(1)}, bf16[1,360,72]{1,2,0:T(8,128)(2,1)}, u32[]{:S(2)}) copy-start(bf16[1,360,72]{1,2,0:T(8,128)(2,1)} %param.11) | copy-start | bytes 155524
  6.5 88.7 %all-gather.2.cloned.1.call-start = ((), (), s32[]{:S(2)}) async-start(), calls=%async_computation | async-start | bytes 2764800 | tf_op jit(solution)/shard_map/all_gather | solution.py:51
  7.4 9.5 %collective-permute-start = (bf16[1,8,72]{1,2,0:T(8,128)(2,1)S(1)}, bf16[1,8,72]{1,2,0:T(8,128)(2,1)S(1)}, u32[]{:S(2)}, u32[]{:S(2)}) collective-permute-start(bf16[1,8,72]{1,2,0:T(8,128)(2,1)S(1)} %get-tuple-element.317), channel_id=1, source_target_pairs={{0,1},{1,2},{2,3},{3,0},{4,5},{5,6},{6,7},{7,4},{8,9},{9,10},{10,1... | collective-permute-start | bytes 3464 | tf_op jit(solution)/shard_map/ppermute | solution.py:20
  10.4 6.5 %collective-permute-start.1 = (bf16[1,8,72]{1,2,0:T(8,128)(2,1)S(1)}, bf16[1,8,72]{1,2,0:T(8,128)(2,1)S(1)}, u32[]{:S(2)}, u32[]{:S(2)}) collective-permute-start(bf16[1,8,72]{1,2,0:T(8,128)(2,1)S(1)} %get-tuple-element.318), channel_id=1, source_target_pairs={{1,0},{2,1},{3,2},{0,3},{5,4},{6,5},{7,6},{4,7},{9,8},{10,9},{11,1... | collective-permute-start | bytes 3464 | tf_op jit(solution)/shard_map/ppermute | solution.py:23
  17.9 15.0 %collective-permute-start.2 = (bf16[1,376,72]{1,2,0:T(8,128)(2,1)S(1)}, bf16[1,376,72]{1,2,0:T(8,128)(2,1)S(1)}, u32[]{:S(2)}, u32[]{:S(2)}) collective-permute-start(bf16[1,376,72]{1,2,0:T(8,128)(2,1)S(1)} %pad_maximum_fusion.4), channel_id=1, source_target_pairs={{0,4},{4,8},{8,12},{12,16},{16,20},{20,24},{24,28},{28,32},{32,36}... | collective-permute-start | bytes 162440 | tf_op jit(solution)/shard_map/ppermute | solution.py:20
  21.0 13.7 %collective-permute-start.3 = (bf16[1,376,72]{1,2,0:T(8,128)(2,1)S(1)}, bf16[1,376,72]{1,2,0:T(8,128)(2,1)S(1)}, u32[]{:S(2)}, u32[]{:S(2)}) collective-permute-start(bf16[1,376,72]{1,2,0:T(8,128)(2,1)S(1)} %pad_maximum_fusion.4), channel_id=1, source_target_pairs={{4,0},{8,4},{12,8},{16,12},{20,16},{24,20},{28,24},{32,28},{36,32}... | collective-permute-start | bytes 162440 | tf_op jit(solution)/shard_map/ppermute | solution.py:23
  38.8 0.7 copy-start.5
  40.4 62.2 %copy-start.6 = (s32[1,1,3,4]{3,1,2,0:T(1,128)S(1)}, s32[1,1,3,4]{3,1,2,0:T(1,128)}, u32[]{:S(2)}) copy-start(s32[1,1,3,4]{3,1,2,0:T(1,128)} %param.19) | copy-start | bytes 148
  95.3 31.5 %copy-start.2 = (bf16[1,1440,768]{2,1,0:T(8,128)(2,1)S(1)}, bf16[1,1440,768]{2,1,0:T(8,128)(2,1)}, u32[]{:S(2)}) copy-start(bf16[1,1440,768]{2,1,0:T(8,128)(2,1)} %all-gather.2.cloned.1.call-done) | copy-start | bytes 6635524
  95.3 29.7 %collective-permute-start.4 = (bf16[1,1440,768]{2,1,0:T(8,128)(2,1)}, bf16[1,1440,768]{2,1,0:T(8,128)(2,1)}, u32[]{:S(2)}, u32[]{:S(2)}) collective-permute-start(bf16[1,1440,768]{2,1,0:T(8,128)(2,1)} %all-gather.2.cloned.1.call-done), channel_id=1, source_target_pairs={{0,4},{4,8},{8,12},{12,16},{16,20},{20,24},{24,28},{28,32},{32,36}... | collective-permute-start | bytes 6635528 | tf_op jit(solution)/shard_map/ppermute | solution.py:20
  100.5 33.1 %collective-permute-start.5 = (bf16[1,1440,768]{2,1,0:T(8,128)(2,1)}, bf16[1,1440,768]{2,1,0:T(8,128)(2,1)}, u32[]{:S(2)}, u32[]{:S(2)}) collective-permute-start(bf16[1,1440,768]{2,1,0:T(8,128)(2,1)} %all-gather.2.cloned.1.call-done), channel_id=1, source_target_pairs={{4,0},{8,4},{12,8},{16,12},{20,16},{24,20},{28,24},{32,28},{36,32}... | collective-permute-start | bytes 6635528 | tf_op jit(solution)/shard_map/ppermute | solution.py:23
  165.9 9.9 %copy-start.4 = (bf16[8,360,48]{1,2,0:T(8,128)(2,1)S(1)}, bf16[8,360,48]{1,2,0:T(8,128)(2,1)}, u32[]{:S(2)}) copy-start(bf16[8,360,48]{1,2,0:T(8,128)(2,1)} %custom-call.4) | copy-start | bytes 829444
  165.9 9.9 %copy-start.7 = (f32[8]{0:T(128)S(1)}, f32[8]{0:T(128)}, u32[]{:S(2)}) copy-start(f32[8]{0:T(128)} %param.18) | copy-start | bytes 100
  175.8 54.0 %copy-start.3 = (bf16[384,384]{1,0:T(8,128)(2,1)S(1)}, bf16[384,384]{1,0:T(8,128)(2,1)}, u32[]{:S(2)}) copy-start(bf16[384,384]{1,0:T(8,128)(2,1)} %param.17) | copy-start | bytes 884740
Sparse Core Ops, SparseCore 0:
  42.6 52.6 all-gather.1
where the time goes:
time: 240 us; the launch traced here: 238 us
  waiting for transfers between devices  80.9 us (34%)
  local copies, waits for them, and re-layouts  58.4 us (24%)
  matrix products  39.3 us (16%)
  other arithmetic  20.6 us (9%)
  starting transfers between devices  18.4 us (8%)
  between operations  14.6 us (6%)
  loops' own time  5.43 us (2%)
    all_gather x1, waiting for transfers between devices, spread(): cycle_cells = lax.all_gather(payload, 'sector', axis=1, tiled=True)  52.8 us
    ppermute x3, waiting for transfers between devices, padded(): lax.ppermute(lax.slice_in_dim(block, block.shape[dim] - width, None, axis...  21.4 us
    dot_general x8, matrix products, one_head(): jnp.dot(expo.astype(jnp.bfloat16), v_head, preferred_element_type=jnp.flo...  17.4 us
    dot_general x8, matrix products, one_head(): jnp.einsum('qd,kd->qk', q_head, k_head, preferred_element_type=jnp.float32)  17 us
    slice x2, local copies, waits for them, and re-layouts, local(): value_all = gathered[..., d_model:].reshape(key_rows, nlon, HEADS, head_dim)  12.1 us
    ppermute x3, starting transfers between devices, padded(): lax.ppermute(lax.slice_in_dim(block, block.shape[dim] - width, None, axis...  11.3 us
    another operation x1, local copies, waits for them, and re-layouts, local(): value_all.reshape(key_rows * nlon, HEADS, head_dim)  9.86 us
    another operation x1, local copies, waits for them, and re-layouts, local(): key_all.reshape(key_rows * nlon, HEADS, head_dim)  9.81 us
  transfers between devices with their start and end apart: 7, of which 3 were waited for; matrix products, arithmetic and copies ran while one was open for 7% of the time, Pallas kernels for 0%

commit v1 on v0

--- a/solution.py
+++ b/solution.py
@@ -48,7 +48,9 @@
 
 
 def spread(payload):
-    cycle_cells = lax.all_gather(payload, "sector", axis=1, tiled=True)
+    cycle_cells = jnp.concatenate(
+        lax.all_to_all(jnp.stack([payload] * lax.axis_size("sector")), "sector", 0, 0), axis=1
+    )
     return padded(cycle_cells, (("band", 0),), KH, False)
 
 

time: 240 us -> 231 us (0.963)
  blocking collectives: 0 us -> 56.6 us
  waiting for transfers between devices: 80.9 us -> 29.8 us
  between operations: 14.6 us -> 1.23 us
  local copies, waits for them, and re-layouts: 58.4 us -> 54.1 us
  other arithmetic: 20.6 us -> 23.8 us
    all_to_all x0 -> x1, blocking collectives: none -> 56.6 us  [spread(): lax.all_to_all(jnp.stack([payload] * lax.axis_size('sector')), 'sector',...]
    all_gather x1 -> x0, waiting for transfers between devices: 52.8 us -> none  [spread(): cycle_cells = lax.all_gather(payload, 'sector', axis=1, tiled=True)]
    concatenate x1 -> x2, other arithmetic: 0.91 us -> 4.13 us  [padded(): block = jnp.concatenate([low, block, high], axis=dim)]
    unnamed x53 -> x49, local copies, waits for them, and re-layouts: 7.28 us -> 5.37 us
  transfers between devices with their start and end apart: 7 -> 6, of which waited for: 3 -> 2; matrix products, arithmetic and copies ran while one was open for 7% -> 7% of each run, Pallas kernels for 0% -> 0%
where the time goes in v1:
time: 231 us; the launch traced here: 228 us
  blocking collectives  56.6 us (25%)
  local copies, waits for them, and re-layouts  54.1 us (23%)
  matrix products  39.3 us (17%)
  waiting for transfers between devices  29.8 us (13%)
  other arithmetic  23.8 us (10%)
  starting transfers between devices  17.9 us (8%)
  loops' own time  5.43 us (2%)
    all_to_all x1, blocking collectives, spread(): lax.all_to_all(jnp.stack([payload] * lax.axis_size('sector')), 'sector',...  56.6 us
    ppermute x3, waiting for transfers between devices, padded(): lax.ppermute(lax.slice_in_dim(block, block.shape[dim] - width, None, axis...  21.1 us
    dot_general x8, matrix products, one_head(): jnp.dot(expo.astype(jnp.bfloat16), v_head, preferred_element_type=jnp.flo...  17.4 us
    dot_general x8, matrix products, one_head(): jnp.einsum('qd,kd->qk', q_head, k_head, preferred_element_type=jnp.float32)  17 us
    slice x2, local copies, waits for them, and re-layouts, local(): value_all = gathered[..., d_model:].reshape(key_rows, nlon, HEADS, head_dim)  12.1 us
    ppermute x3, starting transfers between devices, padded(): lax.ppermute(lax.slice_in_dim(block, block.shape[dim] - width, None, axis...  10.8 us
    another operation x1, local copies, waits for them, and re-layouts, local(): value_all.reshape(key_rows * nlon, HEADS, head_dim)  9.92 us
    another operation x1, local copies, waits for them, and re-layouts, local(): key_all.reshape(key_rows * nlon, HEADS, head_dim)  9.81 us
  transfers between devices with their start and end apart: 6, of which 2 were waited for; matrix products, arithmetic and copies ran while one was open for 7% of the time, Pallas kernels for 0%

profile of v1, /device:TPU:31, one launch (start us, length us, event | category | flops | bytes accessed | tf_op | source)
XLA Modules:
  0.0 228.2 jit_solution(3920541457991879861)
XLA Ops:
  0.9 3.0 %collective-permute-start = (bf16[1,8,72]{1,2,0:T(8,128)(2,1)S(1)}, bf16[1,8,72]{1,2,0:T(8,128)(2,1)S(1)}, u32[]{:S(2)}, u32[]{:S(2)}) collective-permute-start(bf16[1,8,72]{1,2,0:T(8,128)(2,1)S(1)} %get-tuple-element.317), channel_id=1, source_target_pairs={{0,1},{1,2},{2,3},{3,0},{4,5},{5,6},{6,7},{7,4},{8,9},{9,10},{10,1... | collective-permute-start | bytes 3464 | tf_op jit(solution)/shard_map/ppermute | solution.py:20
  3.9 3.1 %collective-permute-start.1 = (bf16[1,8,72]{1,2,0:T(8,128)(2,1)S(1)}, bf16[1,8,72]{1,2,0:T(8,128)(2,1)S(1)}, u32[]{:S(2)}, u32[]{:S(2)}) collective-permute-start(bf16[1,8,72]{1,2,0:T(8,128)(2,1)S(1)} %get-tuple-element.318), channel_id=1, source_target_pairs={{1,0},{2,1},{3,2},{0,3},{5,4},{6,5},{7,6},{4,7},{9,8},{10,9},{11,1... | collective-permute-start | bytes 3464 | tf_op jit(solution)/shard_map/ppermute | solution.py:23
  8.7 1.8 copy.1560
  11.4 3.1 %collective-permute-start.2 = (bf16[1,376,72]{1,2,0:T(8,128)(2,1)S(1)}, bf16[1,376,72]{1,2,0:T(8,128)(2,1)S(1)}, u32[]{:S(2)}, u32[]{:S(2)}) collective-permute-start(bf16[1,376,72]{1,2,0:T(8,128)(2,1)S(1)} %pad_maximum_fusion.4), channel_id=1, source_target_pairs={{0,4},{4,8},{8,12},{12,16},{16,20},{20,24},{24,28},{28,32},{32,36}... | collective-permute-start | bytes 162440 | tf_op jit(solution)/shard_map/ppermute | solution.py:20
  14.4 1.9 collective-permute-start.3
  17.3 0.9 constant_dynamic-update-slice_fusion.32
  18.2 0.9 constant_dynamic-update-slice_fusion.31
  19.1 0.9 constant_dynamic-update-slice_fusion.30
  20.0 0.9 constant_dynamic-update-slice_fusion.29
  29.9 2.3 %fusion.30 = bf16[9,360,72]{1,0,2:T(8,128)(2,1)S(1)} fusion(bf16[1,1,17,360,72]{3,2,1,4,0:T(8,128)(2,1)S(1)} %bitcast.323, bf16[1,1,17,360,72]{3,2,1,4,0:T(8,128)(2,1)S(1)} %bitcast.321, bf16[1,1,17,360,72]{3,2,1,4,0:T(8,128)(2,1)S(1)} %bitcast.322, f32[9,1,3,17]{3,1,2,0:T(1,128)S(1)} %broadcast_multiply_fusion), kind=kOutput, calls=%fused_computation.31 | convolution fusion | flops 145644480 | bytes 3112236 | tf_op jit(solution)/shard_map/kiab,iabjc->kijc/dot_general | solution.py:83
  35.2 56.6 %all_to_all.5 = bf16[4,1,360,768]{3,2,1,0:T(8,128)(2,1)S(1)} all-to-all(bf16[4,1,360,768]{3,2,1,0:T(8,128)(2,1)S(1)} %stack.239), channel_id=1, replica_groups=mesh['band'=64,'sector'=4] {'sector'}, dimensions={0} | all-to-all | bytes 4423680 | tf_op jit(solution)/shard_map/all_to_all | solution.py:52
  91.8 4.7 %collective-permute-start.4 = (bf16[1,1440,768]{2,1,0:T(8,128)(2,1)S(1)}, bf16[1,1440,768]{2,1,0:T(8,128)(2,1)}, u32[]{:S(2)}, u32[]{:S(2)}) collective-permute-start(bf16[1,1440,768]{2,1,0:T(8,128)(2,1)S(1)} %bitcast.315), channel_id=1, source_target_pairs={{0,4},{4,8},{8,12},{12,16},{16,20},{20,24},{24,28},{28,32},{32,36}... | collective-permute-start | bytes 6635528 | tf_op jit(solution)/shard_map/ppermute | solution.py:20
  96.5 2.1 collective-permute-start.5
  98.7 0.9 maximum_bitcast_fusion.7
  99.6 21.1 %collective-permute-done.4 = bf16[1,1440,768]{2,1,0:T(8,128)(2,1)} collective-permute-done((bf16[1,1440,768]{2,1,0:T(8,128)(2,1)S(1)}, bf16[1,1440,768]{2,1,0:T(8,128)(2,1)}, u32[]{:S(2)}, u32[]{:S(2)}) %collective-permute-start.4) | collective-permute-done | bytes 2211872 | tf_op jit(solution)/shard_map/ppermute | solution.py:20
  120.7 8.7 %collective-permute-done.5 = bf16[1,1440,768]{2,1,0:T(8,128)(2,1)} collective-permute-done((bf16[1,1440,768]{2,1,0:T(8,128)(2,1)S(1)}, bf16[1,1440,768]{2,1,0:T(8,128)(2,1)}, u32[]{:S(2)}, u32[]{:S(2)}) %collective-permute-start.5) | collective-permute-done | bytes 2211872 | tf_op jit(solution)/shard_map/ppermute | solution.py:23
  129.4 3.2 %pad_maximum_fusion = bf16[3,1440,768]{2,1,0:T(8,128)(2,1)S(1)} fusion(bf16[1,1440,768]{2,1,0:T(8,128)(2,1)} %collective-permute-done.5, bf16[1,1440,768]{2,1,0:T(8,128)(2,1)S(1)} %bitcast.317, bf16[1,1440,768]{2,1,0:T(8,128)(2,1)} %collective-permute-done.4), kind=kLoop, calls=%fused_computation.19 | loop fusion | flops 6635520 | bytes 13271040 | tf_op jit(solution)/shard_map/concatenate | solution.py:24
  132.7 3.5 %fusion.90 = (bf16[3,1440,384]{2,1,0:T(8,128)(2,1)}, bf16[3,1440,384]{2,1,0:T(8,128)(2,1)}) fusion(bf16[3,1440,768]{2,1,0:T(8,128)(2,1)S(1)} %pad_maximum_fusion), kind=kLoop, calls=%fused_computation.218 | loop fusion | bytes 13271040 | tf_op jit(solution)/shard_map/slice | solution.py:110
  136.1 8.6 %copy.1562 = bf16[3,1440,384]{1,0,2:T(4,128)(2,1)} copy(bf16[3,1440,384]{2,1,0:T(8,128)(2,1)} %get-tuple-element.308) | data formatting | bytes 6635520 | tf_op jit(solution)/shard_map/slice | solution.py:109
  144.8 9.8 %reshape_reshape.7 = bf16[4320,8,48]{0,2,1:T(8,128)(2,1)} reshape(bf16[3,1440,384]{1,0,2:T(4,128)(2,1)} %copy.1562) | data formatting | bytes 6635520 | tf_op jit(solution)/shard_map/reshape;reshape | solution.py:113
  154.6 8.6 %copy.1563 = bf16[3,1440,384]{1,0,2:T(4,128)(2,1)} copy(bf16[3,1440,384]{2,1,0:T(8,128)(2,1)} %get-tuple-element.307) | data formatting | bytes 6635520 | tf_op jit(solution)/shard_map/slice | solution.py:110
  163.2 9.9 %reshape_reshape.8 = bf16[4320,8,48]{0,2,1:T(8,128)(2,1)} reshape(bf16[3,1440,384]{1,0,2:T(4,128)(2,1)} %copy.1563) | data formatting | bytes 6635520 | tf_op jit(solution)/shard_map/reshape;reshape | solution.py:114
  173.1 54.0 %while.11 = (s32[]{:T(128)}, bf16[8,360,48]{1,2,0:T(8,128)(2,1)S(1)}, bf16[8,360,48]{1,2,0:T(8,128)(2,1)S(1)}, bf16[8,4320,48]{1,2,0:T(8,128)(2,1)}, f32[8]{0:T(...) while((s32[]{:T(128)}, ...), condition=%wide.region_4.5_spmd.clone, body=%wide.region_1.4_spmd.clone.sunk | while | flops 309501376 | bytes 19683840 | solution.py:128
  174.5 2.1 fusion.103
  176.7 1.0 fusion.104
  177.7 2.2 fusion.105
  181.3 2.1 fusion.103
  183.4 1.0 fusion.104
  184.4 2.2 fusion.105
  188.0 2.1 fusion.103
  190.2 1.0 fusion.104
  191.2 2.2 fusion.105
  194.8 2.1 fusion.103
  196.9 1.0 fusion.104
  197.9 2.2 fusion.105
  201.5 2.1 fusion.103
  203.7 1.0 fusion.104
  204.7 2.2 fusion.105
  208.3 2.1 fusion.103
  210.4 1.0 fusion.104
  211.4 2.2 fusion.105
  215.0 2.1 fusion.103
  217.1 1.0 fusion.104
  218.1 2.2 fusion.105
  221.8 2.1 fusion.103
  223.9 1.0 fusion.104
  224.9 2.2 fusion.105
  227.1 1.1 fusion.32
  (113 shorter events, 21.5 us)
Async XLA Ops:
  0.0 32.2 %copy-start = (bf16[9,72,384]{2,1,0:T(8,128)(2,1)S(1)}, bf16[9,72,384]{2,1,0:T(8,128)(2,1)}, u32[]{:S(2)}) copy-start(bf16[9,72,384]{2,1,0:T(8,128)(2,1)} %param.14) | copy-start | bytes 1492996
  0.0 25.4 %copy-start.1 = (bf16[1,360,72]{1,2,0:T(8,128)(2,1)S(1)}, bf16[1,360,72]{1,2,0:T(8,128)(2,1)}, u32[]{:S(2)}) copy-start(bf16[1,360,72]{1,2,0:T(8,128)(2,1)} %param.11) | copy-start | bytes 155524
  0.9 9.5 %collective-permute-start = (bf16[1,8,72]{1,2,0:T(8,128)(2,1)S(1)}, bf16[1,8,72]{1,2,0:T(8,128)(2,1)S(1)}, u32[]{:S(2)}, u32[]{:S(2)}) collective-permute-start(bf16[1,8,72]{1,2,0:T(8,128)(2,1)S(1)} %get-tuple-element.317), channel_id=1, source_target_pairs={{0,1},{1,2},{2,3},{3,0},{4,5},{5,6},{6,7},{7,4},{8,9},{9,10},{10,1... | collective-permute-start | bytes 3464 | tf_op jit(solution)/shard_map/ppermute | solution.py:20
  3.9 6.5 %collective-permute-start.1 = (bf16[1,8,72]{1,2,0:T(8,128)(2,1)S(1)}, bf16[1,8,72]{1,2,0:T(8,128)(2,1)S(1)}, u32[]{:S(2)}, u32[]{:S(2)}) collective-permute-start(bf16[1,8,72]{1,2,0:T(8,128)(2,1)S(1)} %get-tuple-element.318), channel_id=1, source_target_pairs={{1,0},{2,1},{3,2},{0,3},{5,4},{6,5},{7,6},{4,7},{9,8},{10,9},{11,1... | collective-permute-start | bytes 3464 | tf_op jit(solution)/shard_map/ppermute | solution.py:23
  11.4 15.0 %collective-permute-start.2 = (bf16[1,376,72]{1,2,0:T(8,128)(2,1)S(1)}, bf16[1,376,72]{1,2,0:T(8,128)(2,1)S(1)}, u32[]{:S(2)}, u32[]{:S(2)}) collective-permute-start(bf16[1,376,72]{1,2,0:T(8,128)(2,1)S(1)} %pad_maximum_fusion.4), channel_id=1, source_target_pairs={{0,4},{4,8},{8,12},{12,16},{16,20},{20,24},{24,28},{28,32},{32,36}... | collective-permute-start | bytes 162440 | tf_op jit(solution)/shard_map/ppermute | solution.py:20
  14.4 13.7 %collective-permute-start.3 = (bf16[1,376,72]{1,2,0:T(8,128)(2,1)S(1)}, bf16[1,376,72]{1,2,0:T(8,128)(2,1)S(1)}, u32[]{:S(2)}, u32[]{:S(2)}) collective-permute-start(bf16[1,376,72]{1,2,0:T(8,128)(2,1)S(1)} %pad_maximum_fusion.4), channel_id=1, source_target_pairs={{4,0},{8,4},{12,8},{16,12},{20,16},{24,20},{28,24},{32,28},{36,32}... | collective-permute-start | bytes 162440 | tf_op jit(solution)/shard_map/ppermute | solution.py:23
  32.2 0.7 copy-start.4
  35.1 63.6 %copy-start.5 = (s32[1,1,3,4]{3,1,2,0:T(1,128)S(1)}, s32[1,1,3,4]{3,1,2,0:T(1,128)}, u32[]{:S(2)}) copy-start(s32[1,1,3,4]{3,1,2,0:T(1,128)} %param.19) | copy-start | bytes 148
  91.8 28.9 %collective-permute-start.4 = (bf16[1,1440,768]{2,1,0:T(8,128)(2,1)S(1)}, bf16[1,1440,768]{2,1,0:T(8,128)(2,1)}, u32[]{:S(2)}, u32[]{:S(2)}) collective-permute-start(bf16[1,1440,768]{2,1,0:T(8,128)(2,1)S(1)} %bitcast.315), channel_id=1, source_target_pairs={{0,4},{4,8},{8,12},{12,16},{16,20},{20,24},{24,28},{28,32},{32,36}... | collective-permute-start | bytes 6635528 | tf_op jit(solution)/shard_map/ppermute | solution.py:20
  96.5 32.9 %collective-permute-start.5 = (bf16[1,1440,768]{2,1,0:T(8,128)(2,1)S(1)}, bf16[1,1440,768]{2,1,0:T(8,128)(2,1)}, u32[]{:S(2)}, u32[]{:S(2)}) collective-permute-start(bf16[1,1440,768]{2,1,0:T(8,128)(2,1)S(1)} %bitcast.316), channel_id=1, source_target_pairs={{4,0},{8,4},{12,8},{16,12},{20,16},{24,20},{28,24},{32,28},{36,32}... | collective-permute-start | bytes 6635528 | tf_op jit(solution)/shard_map/ppermute | solution.py:23
  163.2 9.9 %copy-start.3 = (bf16[8,360,48]{1,2,0:T(8,128)(2,1)S(1)}, bf16[8,360,48]{1,2,0:T(8,128)(2,1)}, u32[]{:S(2)}) copy-start(bf16[8,360,48]{1,2,0:T(8,128)(2,1)} %custom-call.3) | copy-start | bytes 829444
  163.2 9.9 %copy-start.6 = (f32[8]{0:T(128)S(1)}, f32[8]{0:T(128)}, u32[]{:S(2)}) copy-start(f32[8]{0:T(128)} %param.18) | copy-start | bytes 100
  173.1 54.0 %copy-start.2 = (bf16[384,384]{1,0:T(8,128)(2,1)S(1)}, bf16[384,384]{1,0:T(8,128)(2,1)}, u32[]{:S(2)}) copy-start(bf16[384,384]{1,0:T(8,128)(2,1)} %param.17) | copy-start | bytes 884740
